TPU v7x, 32 devices: a whole 2x2x4 slice. The times are simulated.
32 devices in a mesh: dp: 8 (over y, x, core), group: 4 (over z).
Axes of the slice: x: 2, y: 2, z: 4, core: 2. Of those that a mesh axis runs over, the one named last changes fastest.
Arguments:
- inputs: float32 [4096, 768], P(('dp', 'group')), may hold values from -6 to 6
- cotangent: float32 [4096, 768], P(('dp', 'group')), may hold values from -6 to 6
- lengths: int32 [32, 4], P(('dp', 'group')), may hold values from 1 to 64, 128 in all within a row
- attn_weights: float32 [4, 768, 768], P('group', 'dp'), may hold values from -1 to 1
- attn_momenta: float32 [4, 768, 768], P('group', 'dp'), may hold values from -1 to 1
- ffn_weights: float32 [2, 768, 3072], P(None, 'dp', 'group'), may hold values from -1 to 1
- ffn_momenta: float32 [2, 768, 3072], P(None, 'dp', 'group'), may hold values from -1 to 1
- vectors: float32 [12, 768], replicated, may hold values from -2 to 2
- vector_momenta: float32 [12, 768], replicated, may hold values from -1 to 1
Outputs:
- outputs: float32 [4096, 768], P(('dp', 'group'))
- input_grad: float32 [4096, 768], P(('dp', 'group'))
- attn_grads: float32 [4, 768, 768], P('group', 'dp')
- ffn_grads: float32 [2, 768, 3072], P(None, 'dp', 'group')
- vector_grads: float32 [12, 768], replicated
- new_attn_weights: float32 [4, 768, 768], P('group', 'dp')
- new_attn_momenta: float32 [4, 768, 768], P('group', 'dp')
- new_ffn_weights: float32 [2, 768, 3072], P(None, 'dp', 'group')
- new_ffn_momenta: float32 [2, 768, 3072], P(None, 'dp', 'group')
- new_vectors: float32 [12, 768], replicated
- new_vector_momenta: float32 [12, 768], replicated
Inputs may be any that keep to these rules, and one draw needn't show every extreme that they name: Each device's 4 lengths sum to 128.
All inputs are finite; a program needn't handle non-finite values.
Results may differ from a plain program's by a relative error of at most 0.025.
The roundings to bfloat16 on the way count: a program that leaves them out, or rounds other values in their place, can miss the bound.
Values may be sent and summed in bfloat16 or wider, within the bound.
A program may use at most 128 MiB of HBM per device.

v0:
```python
import math

import jax
import jax.numpy as jnp
from jax import lax
from jax.experimental import pallas as pl
from jax.experimental.pallas import tpu as pltpu
from jax.sharding import PartitionSpec as P

HEADS = 12
NS_ITERS = 3


coef_first = 3.4445
coef_second = -4.775
coef_third = 2.0315
momentum_rate = 0.9
muon_rate = 0.8
vector_rate = 0.1


def norm_forward(rows):
    centre = jnp.mean(rows, axis=1, keepdims=True)
    centred = rows - centre
    variance = jnp.mean(centred * centred, axis=1, keepdims=True)
    inverse = lax.rsqrt(variance + 1e-05)
    return (centred * inverse, inverse)


def norm_backward(grad_normed, normed, inverse):
    return inverse * (
        grad_normed
        - jnp.mean(grad_normed, axis=1, keepdims=True)
        - normed * jnp.mean(grad_normed * normed, axis=1, keepdims=True)
    )


def masked_scores(query_heads, key_heads, allowed):
    scores = jnp.einsum("qhd,khd->hqk", query_heads, key_heads, preferred_element_type=jnp.float32)
    return jnp.where(allowed[None], scores, -jnp.inf)


MESH = pl.DeviceIdType.MESH


def flip(index, bits):
    result = index
    for bit in (1, 2, 4):
        if bits & bit:
            result = result + bit - 2 * bit * ((index // bit) % 2)
    return result


def out_struct(kind, x, n_group):
    dtype = x.dtype
    if kind == "zag":
        shape = (n_group,) + x.shape
    elif kind == "za2a":
        shape = x.shape
    elif kind == "dpag":
        shape = (8,) + x.shape
    elif kind == "dprow":
        shape = (x.shape[0], 8 * x.shape[1], x.shape[2])
    elif kind == "dpscatter":
        shape = (x.shape[0], x.shape[1] // 8, x.shape[2])
        dtype = jnp.float32
    else:
        count = kind[1]
        shape = (count, 8 * (n_group // count) * x.shape[0], x.shape[1])
    return jax.ShapeDtypeStruct(shape, dtype)


def scratch_of(kind, x, n_group):
    if kind[0] == "chain":
        return [pltpu.VMEM((n_group,) + x.shape, x.dtype)]
    if kind == "dpscatter":
        count, rows, width = x.shape
        rows = rows // 8
        return [
            pltpu.VMEM((count, 4, rows, width), x.dtype),
            pltpu.VMEM((count, 4, rows, width), x.dtype),
            pltpu.VMEM((count, 4, rows // 2, width), x.dtype),
            pltpu.VMEM((count, 2, rows // 2, width), x.dtype),
            pltpu.VMEM((count, 2, rows // 2, width), x.dtype),
        ]
    return []


def copies_of(kind, x, n_group):
    if kind[0] == "chain":
        return n_group - 1 + 8 * n_group
    if kind == "dprow":
        return 8 * x.shape[0]
    if kind == "dpscatter":
        return 10 * x.shape[0]
    return 7 if kind == "dpag" else n_group - 1


def exchange_kernel(kinds, n_group, scratch_counts, *refs):
    count = len(kinds)
    ins, outs = refs[:count], refs[count : 2 * count]
    send_sem, recv_sem = refs[-2:]
    spare = list(refs[2 * count : -2])
    scratch = []
    for number in scratch_counts:
        scratch.append(spare[:number])
        spare = spare[number:]
    z = lax.axis_index("group")
    d = lax.axis_index("dp")
    z_used = any(kind[0] in ("z", "chain") for kind in kinds)
    dp_used = any(kind[0] in ("d", "chain") for kind in kinds)

    def z_peer(k):
        return lax.rem(z + k, n_group)

    barrier = pltpu.get_barrier_semaphore()
    greeted = 0
    if z_used:
        for k in range(1, n_group):
            pl.semaphore_signal(
                barrier, inc=1, device_id={"group": z_peer(k)}, device_id_type=MESH
            )
            greeted += 1
    if dp_used:
        for k in range(1, 8):
            pl.semaphore_signal(barrier, inc=1, device_id={"dp": flip(d, k)}, device_id_type=MESH)
            greeted += 1
    pl.semaphore_wait(barrier, greeted)

    slot = [0]

    def send(src, dst, device):
        copy = pltpu.make_async_remote_copy(
            src_ref=src,
            dst_ref=dst,
            send_sem=send_sem.at[slot[0]],
            recv_sem=recv_sem.at[slot[0]],
            device_id=device,
            device_id_type=MESH,
        )
        slot[0] += 1
        copy.start()
        return copy

    pending = []
    staged = []

    def spread(src, o, matrix, block, offset, rows):
        first = rows // 32 * 16

        def place(index, part=None):
            start = index * block + offset
            size = rows
            if part is not None:
                start = start + part * first
                size = (first, rows - first)[part]
            return o.at[matrix, pl.ds(pl.multiple_of(start, 16), size), :]

        along_x = send(src, place(d), {"dp": flip(d, 2)})
        along_y = send(src, place(d), {"dp": flip(d, 4)})
        sibling = send(src, place(d), {"dp": flip(d, 1)})
        staged.append((place, along_x, along_y, sibling))

    chained = []
    for kind, x, o, spare in zip(kinds, ins, outs, scratch):
        if kind[0] == "chain":
            copies = [
                send(x, spare[0].at[z], {"group": z_peer(k)}) for k in range(1, n_group)
            ]
            per = n_group // kind[1]
            chained.append((copies, x, o, spare[0], per))
            rows = x.shape[0]
            spread(x, o, z // per, per * rows, lax.rem(z, per) * rows, rows)
    scatters = []
    for kind, x, o, spare in zip(kinds, ins, outs, scratch):
        if kind == "dprow":
            rows = x.shape[1]
            for i in range(x.shape[0]):
                spread(x.at[i], o, i, rows, 0, rows)
        elif kind == "dpscatter":
            rows = x.shape[1] // 8
            for i in range(x.shape[0]):
                copies = []
                for r in (3, 1, 2, 0):
                    start = pl.multiple_of(flip(d, 2 * r + 1) * rows, rows)
                    copies.append(
                        send(
                            x.at[i, pl.ds(start, rows), :],
                            spare[0].at[i, r],
                            {"dp": flip(d, 1)},
                        )
                    )
                scatters.append((i, x, o, rows, spare, copies))
        elif kind == "dpag":
            for k in range(1, 8):
                pending.append(send(x, o.at[d], {"dp": flip(d, k)}))
    if not chained:
        start_z(kinds, ins, outs, z, z_peer, n_group, send, pending)

    for kind, x, o in zip(kinds, ins, outs):
        if kind[0] == "chain":
            per = n_group // kind[1]
            rows = x.shape[0]
            start = pl.multiple_of(d * per * rows + lax.rem(z, per) * rows, 16)
            o[z // per, pl.ds(start, rows), :] = x[...]
        elif kind == "dprow":
            rows = x.shape[1]
            o[:, pl.ds(pl.multiple_of(d * rows, rows), rows), :] = x[...]
        elif kind == "dpag":
            o[d] = x[...]
        elif kind == "zag":
            o[z] = x[...]
        elif kind == "za2a":
            o[z] = x[z]

    for copies, x, o, held, per in chained:
        rows = x.shape[0]
        for k in range(1, n_group):
            copies[k - 1].wait_recv()
            origin = lax.rem(z + n_group - k, n_group)
            offset = lax.rem(origin, per) * rows
            spread(held.at[origin], o, origin // per, per * rows, offset, rows)
            start = pl.multiple_of(d * per * rows + offset, 16)
            o[origin // per, pl.ds(start, rows), :] = held[origin]
    if chained:
        start_z(kinds, ins, outs, z, z_peer, n_group, send, pending)

    second = []
    for place, along_x, along_y, sibling in staged:
        along_x.wait_recv()
        from_x = flip(d, 2)
        to_y = send(place(from_x, 0), place(from_x, 0), {"dp": flip(d, 4)})
        share_x = send(place(from_x), place(from_x), {"dp": flip(d, 1)})
        along_y.wait_recv()
        from_y = flip(d, 4)
        to_x = send(place(from_y, 1), place(from_y, 1), {"dp": flip(d, 2)})
        share_y = send(place(from_y), place(from_y), {"dp": flip(d, 1)})
        second.append((place, (along_x, along_y, to_y, to_x), (sibling, share_x, share_y)))
    third = []
    for place, links, shares in second:
        links[2].wait_recv()
        links[3].wait_recv()
        far = flip(d, 6)
        third.append(send(place(far), place(far), {"dp": flip(d, 1)}))

    wide = jnp.float32
    level = []
    for i, x, o, rows, spare, copies in scatters:
        near, total, recv_b, recv_c, part = spare
        half = rows // 2
        low, high = pl.ds(0, half), pl.ds(half, half)
        for r, copy in zip((3, 1, 2, 0), copies):
            copy.wait_recv()
            start = pl.multiple_of(flip(d, 2 * r) * rows, rows)
            own = x[i, pl.ds(start, rows), :].astype(wide)
            total[i, r] = (own + near[i, r].astype(wide)).astype(total.dtype)
        to_x = {"dp": flip(d, 2)}
        to_y = {"dp": flip(d, 4)}
        moved = [
            send(total.at[i, 3, low], recv_b.at[i, 1], to_x),
            send(total.at[i, 3, high], recv_b.at[i, 3], to_y),
            send(total.at[i, 1, low], recv_b.at[i, 0], to_x),
            send(total.at[i, 2, high], recv_b.at[i, 2], to_y),
        ]
        level.append(moved)
    last = []
    for (i, x, o, rows, spare, copies), moved in zip(scatters, level):
        near, total, recv_b, recv_c, part = spare
        half = rows // 2
        low, high = pl.ds(0, half), pl.ds(half, half)
        moved[0].wait_recv()
        part[i, 0] = (
            total[i, 2, low].astype(wide) + recv_b[i, 1].astype(wide)
        ).astype(part.dtype)
        moved[1].wait_recv()
        part[i, 1] = (
            total[i, 1, high].astype(wide) + recv_b[i, 3].astype(wide)
        ).astype(part.dtype)
        last.append(
            (
                send(part.at[i, 0], recv_c.at[i, 0], {"dp": flip(d, 4)}),
                send(part.at[i, 1], recv_c.at[i, 1], {"dp": flip(d, 2)}),
            )
        )
    for (i, x, o, rows, spare, copies), moved, ends in zip(scatters, level, last):
        near, total, recv_b, recv_c, part = spare
        half = rows // 2
        low, high = pl.ds(0, half), pl.ds(half, half)
        moved[2].wait_recv()
        moved[3].wait_recv()
        ends[0].wait_recv()
        o[i, low, :] = (
            total[i, 0, low].astype(wide) + recv_b[i, 0].astype(wide) + recv_c[i, 0].astype(wide)
        )
        ends[1].wait_recv()
        o[i, high, :] = (
            total[i, 0, high].astype(wide) + recv_b[i, 2].astype(wide) + recv_c[i, 1].astype(wide)
        )
        for copy in (*copies, *moved, *ends):
            copy.wait_send()

    for copies, *_ in chained:
        for copy in copies:
            copy.wait_send()
    for place, links, shares in second:
        for copy in shares:
            copy.wait()
        for copy in links:
            copy.wait_send()
    for copy in third:
        copy.wait()
    for copy in pending:
        copy.wait()


def start_z(kinds, ins, outs, z, z_peer, n_group, send, pending):
    for kind, x, o in zip(kinds, ins, outs):
        for k in range(1, n_group):
            if kind == "zag":
                pending.append(send(x, o.at[z], {"group": z_peer(k)}))
            elif kind == "za2a":
                pending.append(send(x.at[z_peer(k)], o.at[z], {"group": z_peer(k)}))


def exchange(collective_id, *pairs):
    n_group = lax.axis_size("group")
    kinds = tuple(kind for kind, _ in pairs)
    arrays = [x for _, x in pairs]
    if lax.axis_size("dp") != 8:
        results = []
        for kind, x in pairs:
            if kind == "zag":
                results.append(lax.all_gather(x, "group", axis=0))
            elif kind == "za2a":
                results.append(lax.all_to_all(x, "group", 0, 0))
            elif kind == "dpag":
                results.append(lax.all_gather(x, "dp", axis=0))
            elif kind == "dprow":
                results.append(lax.all_gather(x, "dp", axis=1, tiled=True))
            elif kind == "dpscatter":
                wide = x.astype(jnp.float32)
                results.append(lax.psum_scatter(wide, "dp", scatter_dimension=1, tiled=True))
            else:
                held = lax.all_gather(x, "group", axis=0).reshape(kind[1], -1, x.shape[1])
                results.append(lax.all_gather(held, "dp", axis=1, tiled=True))
        return results
    copies = sum(copies_of(kind, x, n_group) for kind, x in pairs)
    scratch = [scratch_of(kind, x, n_group) for kind, x in pairs]
    scratch_counts = tuple(len(shapes) for shapes in scratch)
    return pl.pallas_call(
        lambda *refs: exchange_kernel(kinds, n_group, scratch_counts, *refs),
        out_shape=[out_struct(kind, x, n_group) for kind, x in pairs],
        in_specs=[pl.BlockSpec(memory_space=pltpu.VMEM)] * len(kinds),
        out_specs=[pl.BlockSpec(memory_space=pltpu.VMEM)] * len(kinds),
        scratch_shapes=[
            *[shape for shapes in scratch for shape in shapes],
            pltpu.SemaphoreType.DMA((copies,)),
            pltpu.SemaphoreType.DMA((copies,)),
        ],
        compiler_params=pltpu.CompilerParams(collective_id=collective_id, has_side_effects=True),
        name=f"exchange_{collective_id}",
    )(*arrays)


def mm(left, right, dims):
    return lax.dot_general(left, right, (dims, ((), ())), preferred_element_type=jnp.float32)


NN = ((1,), (0,))
NT = ((1,), (1,))
TN = ((0,), (0,))


def newton_schulz_rows(gram, own_rows, whole_b, row_start):
    rows = own_rows.shape[0]
    lead = 1.0
    spread = None
    for iteration in range(NS_ITERS - 1):
        gram_b = gram.astype(jnp.bfloat16)
        mixed = coef_second * gram + coef_third * mm(gram_b, gram_b, NN)
        mixed_b = mixed.astype(jnp.bfloat16)
        half = coef_first * gram + mm(mixed_b, gram_b, NN)
        gram = coef_first * half + mm(half.astype(jnp.bfloat16), mixed_b, NN)
        mine = lax.dynamic_slice_in_dim(mixed, row_start, rows, 0)
        if spread is None:
            spread = mine
        else:
            product = mm(spread.astype(jnp.bfloat16), mixed_b, NN)
            spread = coef_first * spread + lead * mine + product
        lead = lead * coef_first
    gram_b = gram.astype(jnp.bfloat16)
    once = lead * lax.dynamic_slice_in_dim(gram, row_start, rows, 0) + mm(
        spread.astype(jnp.bfloat16), gram_b, NN
    )
    twice = mm(once.astype(jnp.bfloat16), gram_b, NN)
    spread = coef_first * spread + coef_second * once + coef_third * twice
    lead = lead * coef_first
    return lead * own_rows + mm(spread.astype(jnp.bfloat16), whole_b, NN)


def on_device(
    inputs,
    cotangent,
    lengths,
    attn_weights,
    attn_momenta,
    ffn_weights,
    ffn_momenta,
    vectors,
    vector_momenta,
):
    group_count = lax.axis_size("group")
    dp_count = lax.axis_size("dp")
    own_index = lax.axis_index("group")
    dp_index = lax.axis_index("dp")
    token_count, width = inputs.shape
    own_count = attn_weights.shape[1]
    quarter = ffn_weights.shape[2]
    head_size = width // HEADS
    scale = 1.0 / math.sqrt(head_size)
    bf16 = jnp.bfloat16

    own_attn = attn_weights.astype(bf16)
    own_ffn = ffn_weights.astype(bf16)
    cotan_b = cotangent.astype(bf16)
    attn_full, ffn_full, all_cotan = exchange(
        0, (("chain", 4), own_attn[0]), ("dprow", own_ffn), ("zag", cotan_b)
    )
    w_query, w_key, w_value, w_output = [attn_full[i] for i in range(4)]
    w_expand, w_reduce = [ffn_full[i] for i in range(2)]
    all_cotan = all_cotan.reshape(-1, width)

    positions = jnp.arange(token_count, dtype=jnp.int32)
    seq_ends = jnp.cumsum(lengths[0])
    segment = jnp.sum((positions[:, None] >= seq_ends[None, :]).astype(jnp.int32), axis=1)
    allowed = (segment[:, None] == segment[None, :]) & (positions[None, :] <= positions[:, None])
    normed_first, inverse_first = norm_forward(inputs)
    hidden_first = (normed_first * vectors[0] + vectors[1]).astype(bf16)
    query = ((mm(hidden_first, w_query, NN) + vectors[2]) * scale).astype(bf16)
    keyed = mm(hidden_first, w_key, NN).astype(bf16)
    valued = (mm(hidden_first, w_value, NN) + vectors[3]).astype(bf16)
    query_heads = query.reshape(token_count, HEADS, head_size)
    key_heads = keyed.reshape(token_count, HEADS, head_size)
    value_heads = valued.reshape(token_count, HEADS, head_size)
    scores = masked_scores(query_heads, key_heads, allowed)
    highest = jnp.max(scores, axis=2, keepdims=True)
    log_total = highest + jnp.log(jnp.sum(jnp.exp(scores - highest), axis=2, keepdims=True))
    probs = jnp.exp(scores - log_total)
    probs_b = probs.astype(bf16)
    attended = jnp.einsum("hqk,khd->qhd", probs_b, value_heads, preferred_element_type=jnp.float32)
    attended = attended.reshape(token_count, width).astype(bf16)
    middle = inputs + mm(attended, w_output, NN) + vectors[4]
    normed_second, inverse_second = norm_forward(middle)
    hidden_second = (normed_second * vectors[5] + vectors[6]).astype(bf16)

    (all_second,) = exchange(2, ("zag", hidden_second))
    all_second = all_second.reshape(-1, width)
    own_bias = lax.dynamic_slice_in_dim(vectors[8:].reshape(-1), own_index * quarter, quarter, 0)
    before = mm(all_second, w_expand, NN) + own_bias
    active = jnp.maximum(before, 0.0).astype(bf16)
    out_part = mm(active, w_reduce, NT).astype(bf16)
    grad_before = jnp.where(before > 0.0, mm(all_cotan, w_reduce, NN), 0.0)
    before_grad_b = grad_before.astype(bf16)
    second_part = mm(before_grad_b, w_expand, NT).astype(bf16)

    (second_parts,) = exchange(
        3, ("za2a", second_part.reshape(group_count, token_count, width))
    )
    grad_second = jnp.sum(second_parts.astype(jnp.float32), axis=0)
    grad_middle = cotangent + norm_backward(
        grad_second * vectors[5], normed_second, inverse_second
    )
    middle_b = grad_middle.astype(bf16)
    grad_attended = mm(middle_b, w_output, NT).astype(bf16)
    attended_heads = grad_attended.reshape(token_count, HEADS, head_size)
    grad_probs = jnp.einsum(
        "qhd,khd->hqk", attended_heads, value_heads, preferred_element_type=jnp.float32
    )
    grad_value = jnp.einsum(
        "hqk,qhd->khd", probs_b, attended_heads, preferred_element_type=jnp.float32
    )
    delta = jnp.sum(probs * grad_probs, axis=2, keepdims=True)
    grad_scores = (probs * (grad_probs - delta)).astype(bf16)
    grad_query = (
        jnp.einsum("hqk,khd->qhd", grad_scores, key_heads, preferred_element_type=jnp.float32)
        * scale
    )
    grad_key = jnp.einsum(
        "hqk,qhd->khd", grad_scores, query_heads, preferred_element_type=jnp.float32
    )
    query_grad = grad_query.reshape(token_count, width)
    key_grad = grad_key.reshape(token_count, width)
    value_grad = grad_value.reshape(token_count, width)
    query_grad_b = query_grad.astype(bf16)
    key_grad_b = key_grad.astype(bf16)
    value_grad_b = value_grad.astype(bf16)

    ffn_terms = jnp.stack(
        [mm(all_second, before_grad_b, TN).astype(bf16), mm(all_cotan, active, TN).astype(bf16)]
    )
    left, right, ffn_total = exchange(
        4,
        ("za2a", jnp.stack([hidden_first, hidden_first, hidden_first, attended])),
        ("za2a", jnp.stack([query_grad_b, key_grad_b, value_grad_b, middle_b])),
        ("dpscatter", ffn_terms),
    )
    grad_first = (
        mm(query_grad_b, w_query, NT) + mm(key_grad_b, w_key, NT) + mm(value_grad_b, w_value, NT)
    )
    input_grad = grad_middle + norm_backward(grad_first * vectors[0], normed_first, inverse_first)
    small_terms = jnp.stack(
        [
            jnp.sum(grad_first * normed_first, axis=0),
            jnp.sum(grad_first, axis=0),
            jnp.sum(query_grad, axis=0),
            jnp.sum(value_grad, axis=0),
            jnp.sum(grad_middle, axis=0),
            jnp.sum(grad_second * normed_second, axis=0),
            jnp.sum(grad_second, axis=0),
            jnp.sum(cotangent, axis=0),
        ]
    )
    owner_mask = jnp.arange(group_count, dtype=jnp.int32) == own_index
    bias_terms = jnp.where(owner_mask[:, None], jnp.sum(grad_before, axis=0)[None], 0.0)
    vector_terms = jnp.concatenate([small_terms, bias_terms.reshape(-1, width)], axis=0)
    attn_term = mm(left.reshape(-1, width), right.reshape(-1, width), TN).astype(bf16)
    vector_all, attn_total = exchange(5, ("dpag", vector_terms), ("dpscatter", attn_term[None]))
    total_tokens = float(token_count * dp_count * group_count)
    attn_grads = attn_total / total_tokens
    ffn_grads = ffn_total / total_tokens
    attn_next = momentum_rate * attn_momenta + attn_grads
    ffn_next = momentum_rate * ffn_momenta + ffn_grads
    own_next = jnp.concatenate([attn_next, ffn_next], axis=0)
    squares = jnp.sum(own_next * own_next, axis=(1, 2))
    squares = jnp.broadcast_to(jnp.pad(squares, (0, 5))[:, None], (8, 128))

    next_full, square_all, vector_groups, out_parts = exchange(
        6,
        ("dprow", own_next.astype(bf16)),
        ("dpag", squares),
        ("zag", jnp.sum(vector_all, axis=0)),
        ("za2a", out_part.reshape(group_count, token_count, width)),
    )
    outputs = middle + jnp.sum(out_parts.astype(jnp.float32), axis=0) + vectors[7]
    square_plane = jnp.sum(square_all, axis=0)
    own_b = own_next.astype(bf16)
    gram_part = jnp.concatenate([mm(own_b[1], next_full[1], NT), mm(own_b[2], next_full[2], NT)])
    piece = 2 * own_count // group_count
    gram_pieces, square_groups = exchange(
        7,
        ("za2a", gram_part.astype(bf16).reshape(group_count, piece, width)),
        ("zag", square_plane),
    )
    ffn_square = jnp.sum(square_groups, axis=0)[1:3, 0]
    attn_scale = 1.0 / (jnp.sqrt(square_plane[0, 0]) + 1e-07)
    ffn_scale = 1.0 / (jnp.sqrt(ffn_square) + 1e-07)
    piece_scale = jnp.where(own_index < group_count // 2, ffn_scale[0], ffn_scale[1])
    gram_piece = (jnp.sum(gram_pieces.astype(jnp.float32), axis=0) * (piece_scale * piece_scale)).astype(bf16)
    (gram_full,) = exchange(8, (("chain", 2), gram_piece))

    row_start = dp_index * own_count
    attn_unit = next_full[0].astype(jnp.float32) * attn_scale
    attn_unit_b = attn_unit.astype(bf16)
    attn_gram = mm(attn_unit_b, attn_unit_b, NT)
    steps = [newton_schulz_rows(attn_gram, own_next[0] * attn_scale, attn_unit_b, row_start)]
    for i in range(2):
        unit_b = (next_full[1 + i].astype(jnp.float32) * ffn_scale[i]).astype(bf16)
        steps.append(
            newton_schulz_rows(
                gram_full[i].astype(jnp.float32), own_next[1 + i] * ffn_scale[i], unit_b, row_start
            )
        )
    new_attn_weights = attn_weights - muon_rate * steps[0][None]
    new_ffn_weights = ffn_weights - muon_rate * jnp.stack(steps[1:])
    vector_grads = jnp.sum(vector_groups, axis=0) / total_tokens
    new_vector_momenta = momentum_rate * vector_momenta + vector_grads
    mean_square = jnp.mean(new_vector_momenta * new_vector_momenta, axis=1, keepdims=True)
    new_vectors = vectors - vector_rate * new_vector_momenta * lax.rsqrt(mean_square + 1e-06)
    return (
        outputs,
        input_grad,
        attn_grads,
        ffn_grads,
        vector_grads,
        new_attn_weights,
        attn_next,
        new_ffn_weights,
        ffn_next,
        new_vectors,
        new_vector_momenta,
    )


def solution(mesh):
    in_specs = (
        P(("dp", "group"), None),
        P(("dp", "group"), None),
        P(("dp", "group"), None),
        P("group", "dp", None),
        P("group", "dp", None),
        P(None, "dp", "group"),
        P(None, "dp", "group"),
        P(),
        P(),
    )
    out_specs = (
        P(("dp", "group"), None),
        P(("dp", "group"), None),
        P("group", "dp", None),
        P(None, "dp", "group"),
        P(),
        P("group", "dp", None),
        P("group", "dp", None),
        P(None, "dp", "group"),
        P(None, "dp", "group"),
        P(),
        P(),
    )
    return jax.shard_map(
        on_device, mesh=mesh, in_specs=in_specs, out_specs=out_specs, check_vma=False
    )
```

profile of v0, /device:TPU:0, one launch (start us, length us, event | category | flops | bytes accessed | tf_op | source)
XLA Modules:
  0.0 334.7 jit_solution(6073623061117216049)
XLA Ops:
  0.7 1.7 slice_reduce_fusion
  3.5 1.2 multiply_reduce_fusion.7
  4.7 2.4 fusion.187
  7.1 1.8 convert_element_type.284.refs_1_
  9.6 41.6 %exchange_0.1 = (bf16[4,768,768]{2,1,0:T(8,128)(2,1)}, bf16[2,768,768]{2,1,0:T(8,128)(2,1)}, bf16[4,128,768]{2,1,0:T(8,128)(2,1)}) custom-call(bf16[96,768]{1,0:T(8,128)(2,1)} %convert_bitcast_fusion.refs_0_, bf16[2,96,768]{2,1,0:T(8,128)(2,1)} %convert_element_type.284.refs_1_, bf16[128,768]{1,0:T(8,128)(2,1)} %get-tuple-element.68.refs_2_), custom_call_target="tpu_custom_call" | custom-call | tf_op jit(solution)/shard_map/exchange_0/pallas_call | solution.py:350
  51.2 1.7 fusion.46
  53.1 1.6 fusion.49
  55.8 1.6 fusion.55
  57.8 1.7 fusion.192
  60.6 19.5 %exchange_2.1 = bf16[4,128,768]{2,1,0:T(8,128)(2,1)} custom-call(bf16[128,768]{1,0:T(8,128)(2,1)} %add_convert_fusion.refs_0_), custom_call_target="tpu_custom_call" | custom-call | tf_op jit(solution)/shard_map/exchange_2/pallas_call | solution.py:350
  80.2 2.4 convolution_add_fusion
  82.7 1.4 fusion.193
  86.0 1.7 pad_maximum_fusion.refs_2_
  87.7 1.7 convolution_convert_fusion.3
  89.4 21.5 %exchange_3.1 = bf16[4,128,768]{2,1,0:T(8,128)(2,1)} custom-call(bf16[4,128,768]{2,1,0:T(8,128)(2,1)} %bitcast.201), custom_call_target="tpu_custom_call" | custom-call | tf_op jit(solution)/shard_map/exchange_3/pallas_call | solution.py:350
  110.9 1.5 convert_reduce_fusion
  113.5 1.8 fusion.52
  117.2 1.8 fusion.33
  119.0 1.8 convolution_add_fusion.2
  120.9 1.9 multiply_reduce_fusion.2
  126.5 41.1 %exchange_4.1 = (bf16[4,128,768]{2,1,0:T(8,128)(2,1)}, bf16[4,128,768]{2,1,0:T(8,128)(2,1)}, f32[2,96,768]{2,1,0:T(8,128)}) custom-call(bf16[4,128,768]{2,1,0:T(8,128)(2,1)} %pad_maximum_fusion.2.refs_0_, bf16[4,128,768]{2,1,0:T(8,128)(2,1)} %pad_maximum_fusion.3.refs_1_, bf16[2,768,768]{2,1,0:T(8,128)(2,1)} %pad_maximum_fusion.refs_2_), custom_call_target="tpu_custom_call" | custom-call | tf_op jit(solution)/shard_map/exchange_4/pallas_call | solution.py:350
  167.6 3.2 fusion.6.refs_1_
  171.2 1.3 concatenate.10.refs_0_
  172.4 16.8 %exchange_5.1 = (f32[8,12,768]{2,1,0:T(8,128)}, f32[1,96,768]{2,1,0:T(8,128)}) custom-call(f32[12,768]{1,0:T(8,128)} %concatenate.10.refs_0_, bf16[1,768,768]{2,1,0:T(8,128)(2,1)} %fusion.6.refs_1_), custom_call_target="tpu_custom_call" | custom-call | tf_op jit(solution)/shard_map/exchange_5/pallas_call | solution.py:350
  189.2 1.7 multiply_add_fusion.17
  191.0 2.3 multiply_add_fusion.14
  195.6 3.0 convolution_convert_fusion.2
  198.6 28.0 %exchange_6.1 = (bf16[3,768,768]{2,1,0:T(8,128)(2,1)}, f32[8,8,128]{2,1,0:T(8,128)}, f32[4,12,768]{2,1,0:T(8,128)}, bf16[4,128,768]{2,1,0:T(8,128)(2,1)}) custom-call(bf16[3,96,768]{2,1,0:T(8,128)(2,1)} %fusion.100.refs_0_, f32[8,128]{1,0:T(8,128)} %broadcast_in_dim.37.refs_1_, f32[12,768]{1,0:T(8,128)} %reduce_sum.281.refs_2_, bf16[4,128,768]{2,1,0:T(8,128)(2,1)} %bitcast.200), custom_call_target="tpu_custom_call" | custom-call | tf_op jit(solution)/shard_map/exchange_6/pallas_call | solution.py:350
  226.6 1.8 fusion.68
  228.4 1.8 fusion.71
  231.5 13.0 %exchange_7.1 = (bf16[4,48,768]{2,1,0:T(8,128)(2,1)}, f32[4,8,128]{2,1,0:T(8,128)}) custom-call(bf16[4,48,768]{2,1,0:T(8,128)(2,1)} %bitcast.195, f32[8,128]{1,0:T(8,128)} %reduce_sum.286.refs_1_), custom_call_target="tpu_custom_call" | custom-call | tf_op jit(solution)/shard_map/exchange_7/pallas_call | solution.py:350
  248.7 22.2 %exchange_8.1 = bf16[2,768,768]{2,1,0:T(8,128)(2,1)} custom-call(bf16[48,768]{1,0:T(8,128)(2,1)} %multiply_convert_fusion.14.refs_0_), custom_call_target="tpu_custom_call" | custom-call | tf_op jit(solution)/shard_map/exchange_8/pallas_call | solution.py:350
  270.9 3.2 fusion
  276.8 1.4 copy-done.2
  278.2 1.1 multiply_add_fusion.6
  279.3 1.5 convolution_add_fusion.9
  283.4 1.4 copy-done
  285.8 4.4 %fusion.61 = f32[1,96,768]{2,1,0:T(8,128)} fusion(f32[]{:T(128)} %bitcast.44, bf16[3,768,768]{2,1,0:T(8,128)(2,1)} %get-tuple-element.36, f32[768,768]{1,0:T(8,128)} %copy-done, f32[2,96,768]{2,1,0:T(8,128)S(1)} %get-tuple-element.63, f32[96,768]{1,0:T(8,128)} %convolution_add_fusion.8, f32[96,768]{1,0:T(8,128)} %copy-done.8), kind=kOutput, calls=%fused_computation.96 | convolution fusion | flops 229588992 | bytes 5014528 | tf_op jit(solution)/shard_map/dot_general | solution.py:366
  290.3 10.7 %fusion.2 = f32[768,768]{1,0:T(8,128)S(1)} fusion(bf16[2,768,768]{2,1,0:T(8,128)(2,1)S(1)} %copy-done.11), kind=kOutput, calls=%fused_computation.6 | convolution fusion | flops 908328960 | bytes 4718592 | tf_op jit(solution)/shard_map/dot_general | solution.py:366
  303.2 1.1 multiply_add_fusion.2
  308.0 3.6 %fusion.59 = f32[1,96,768]{2,1,0:T(8,128)} fusion(f32[]{:T(128)} %bitcast.46, bf16[3,768,768]{2,1,0:T(8,128)(2,1)} %get-tuple-element.36, f32[768,768]{1,0:T(8,128)S(1)} %multiply_add_fusion, f32[2,96,768]{2,1,0:T(8,128)S(1)} %get-tuple-element.63, f32[96,768]{1,0:T(8,128)} %convolution_add_fusion.6, f32[96,768]{1,0:T(8,128)} %copy-done.9), kind=kOutput, calls=%fused_computation.94 | convolution fusion | flops 229588992 | bytes 5014528 | tf_op jit(solution)/shard_map/dot_general | solution.py:366
  311.6 2.1 fusion.102
  313.7 1.5 multiply_reduce_fusion.10
  315.3 1.5 multiply_subtract_fusion
  316.8 1.2 slice.109
  318.7 2.8 fusion.98
  329.6 2.8 fusion.67
  332.4 1.3 convert_reduce_fusion.2
  (159 shorter events, 40.6 us)
Async XLA Ops:
  0.6 50.6 %copy-start.1 = (f32[128,768]{1,0:T(8,128)S(1)}, f32[128,768]{1,0:T(8,128)}, u32[]{:S(2)}) copy-start(f32[128,768]{1,0:T(8,128)} %param.9) | copy-start | bytes 1179652
  0.7 8.3 %copy-start.16 = (f32[1,96,768]{2,1,0:T(8,128)S(1)}, f32[1,96,768]{2,1,0:T(8,128)}, u32[]{:S(2)}) copy-start(f32[1,96,768]{2,1,0:T(8,128)} %param.12) | copy-start | bytes 884740
  2.4 53.4 %copy-start.25 = (f32[768]{0:T(1024)}, f32[768]{0:T(1024)S(1)}, u32[]{:S(2)}) copy-start(f32[768]{0:T(1024)S(1)} %get-tuple-element.54) | copy-start | bytes 9220
  3.5 52.3 %copy-start.30 = (f32[128]{0:T(128)}, f32[128]{0:T(128)S(1)}, u32[]{:S(2)}) copy-start(f32[128]{0:T(128)S(1)} %broadcast_multiply_fusion.8) | copy-start | bytes 1540
  4.7 51.1 %copy-start.33 = (f32[128]{0:T(128)}, f32[128]{0:T(128)S(1)}, u32[]{:S(2)}) copy-start(f32[128]{0:T(128)S(1)} %add_rsqrt_fusion.1) | copy-start | bytes 1540
  51.2 3.7 %copy-start.36 = (s32[1,4]{1,0:T(1,128)S(1)}, s32[1,4]{1,0:T(1,128)}, u32[]{:S(2)}) copy-start(s32[1,4]{1,0:T(1,128)} %param.11) | copy-start | bytes 52
  57.8 22.3 %slice-start = ((f32[12,768]{1,0:T(8,128)}), f32[4,768]{1,0:T(4,128)S(1)}, s32[]{:S(2)}) async-start(f32[12,768]{1,0:T(8,128)} %param.16), calls=%async_computation | async-start | bytes 24576 | tf_op jit(solution)/shard_map/slice | solution.py:458
  59.6 52.8 %copy-start.28 = (f32[128]{0:T(128)}, f32[128]{0:T(128)S(1)}, u32[]{:S(2)}) copy-start(f32[128]{0:T(128)S(1)} %broadcast_multiply_fusion.7) | copy-start | bytes 1540
  59.8 52.6 %copy-start.29 = (f32[128]{0:T(128)}, f32[128]{0:T(128)S(1)}, u32[]{:S(2)}) copy-start(f32[128]{0:T(128)S(1)} %add_rsqrt_fusion) | copy-start | bytes 1540
  80.1 2.6 copy-start.17
  80.1 2.6 copy-start.35
  82.6 2.5 copy-start.13
  82.7 1.7 copy-start.18
  89.4 23.3 %copy-start.15 = (f32[128,768]{1,0:T(8,128)S(1)}, f32[128,768]{1,0:T(8,128)}, u32[]{:S(2)}) copy-start(f32[128,768]{1,0:T(8,128)} %param.10) | copy-start | bytes 1179652
  116.9 4.0 %copy-start.31 = (f32[128]{0:T(128)S(1)}, f32[128]{0:T(128)}, u32[]{:S(2)}) copy-start(f32[128]{0:T(128)} %copy-done.30) | copy-start | bytes 1540
  116.9 4.0 %copy-start.34 = (f32[128]{0:T(128)S(1)}, f32[128]{0:T(128)}, u32[]{:S(2)}) copy-start(f32[128]{0:T(128)} %copy-done.33) | copy-start | bytes 1540
  122.8 2.5 copy-start.26
  167.6 3.5 %copy-start.32 = (f32[768]{0:T(1024)S(1)}, f32[768]{0:T(1024)}, u32[]{:S(2)}) copy-start(f32[768]{0:T(1024)} %get-tuple-element.84) | copy-start | bytes 9220
  167.6 3.5 %copy-start.27 = (f32[768]{0:T(1024)S(1)}, f32[768]{0:T(1024)}, u32[]{:S(2)}) copy-start(f32[768]{0:T(1024)} %get-tuple-element.67) | copy-start | bytes 9220
  167.6 21.6 %copy-start.20 = (f32[1,96,768]{2,1,0:T(8,128)S(1)}, f32[1,96,768]{2,1,0:T(8,128)}, u32[]{:S(2)}) copy-start(f32[1,96,768]{2,1,0:T(8,128)} %param.13) | copy-start | bytes 884740
  191.0 3.2 copy-start.5
  191.0 4.0 %copy-start.19 = (f32[8,12,768]{2,1,0:T(8,128)S(1)}, f32[8,12,768]{2,1,0:T(8,128)}, u32[]{:S(2)}) copy-start(f32[8,12,768]{2,1,0:T(8,128)} %get-tuple-element.32) | copy-start | bytes 884740
  191.0 4.6 %copy-start.14 = (f32[512,768]{1,0:T(8,128)S(1)}, f32[512,768]{1,0:T(8,128)}, u32[]{:S(2)}) copy-start(f32[512,768]{1,0:T(8,128)} %copy-done.13) | copy-start | bytes 4718596
  193.3 114.7 %copy-start.4 = (f32[2,96,768]{2,1,0:T(8,128)}, f32[2,96,768]{2,1,0:T(8,128)S(1)}, u32[]{:S(2)}) copy-start(f32[2,96,768]{2,1,0:T(8,128)S(1)} %get-tuple-element.63) | copy-start | bytes 1769476
  195.6 31.0 %copy-start.12 = (bf16[3,96,768]{2,1,0:T(8,128)(2,1)S(1)}, bf16[3,96,768]{2,1,0:T(8,128)(2,1)}, u32[]{:S(2)}) copy-start(bf16[3,96,768]{2,1,0:T(8,128)(2,1)} %fusion.100.refs_0_) | copy-start | bytes 1327108
  226.6 4.3 %copy-start.23 = (f32[8,8,128]{2,1,0:T(8,128)S(1)}, f32[8,8,128]{2,1,0:T(8,128)}, u32[]{:S(2)}) copy-start(f32[8,8,128]{2,1,0:T(8,128)} %get-tuple-element.35) | copy-start | bytes 98308
  270.9 3.3 copy-start.10
  274.2 1.5 copy-start.7
  276.7 1.4 copy-start.2
  279.3 1.8 copy-start.3
  281.1 2.2 copy-start.8
  283.4 1.4 copy-start
  285.8 4.4 %copy-start.11 = (bf16[2,768,768]{2,1,0:T(8,128)(2,1)S(1)}, bf16[2,768,768]{2,1,0:T(8,128)(2,1)}, u32[]{:S(2)}) copy-start(bf16[2,768,768]{2,1,0:T(8,128)(2,1)} %exchange_8.1) | copy-start | bytes 7077892
  304.7 2.2 copy-start.9
  308.0 5.7 %copy-start.21 = (f32[4,12,768]{2,1,0:T(8,128)S(1)}, f32[4,12,768]{2,1,0:T(8,128)}, u32[]{:S(2)}) copy-start(f32[4,12,768]{2,1,0:T(8,128)} %get-tuple-element.34) | copy-start | bytes 442372
  315.3 6.2 %copy-start.22 = (f32[12,768]{1,0:T(8,128)}, f32[12,768]{1,0:T(8,128)S(1)}, u32[]{:S(2)}) copy-start(f32[12,768]{1,0:T(8,128)S(1)} %get-tuple-element.57) | copy-start | bytes 110596
  328.5 1.1 copy-start.6
  329.6 4.1 %copy-start.24 = (f32[768]{0:T(1024)S(1)}, f32[768]{0:T(1024)}, u32[]{:S(2)}) copy-start(f32[768]{0:T(1024)} %get-tuple-element.48) | copy-start | bytes 9220
where the time goes:
time: 340 us; the launch traced here: 335 us
  Pallas kernels  204 us (60%)
  matrix products  83.7 us (25%)
  other arithmetic  32.9 us (10%)
  local copies, waits for them, and re-layouts  10.7 us (3%)
  between operations  3.81 us (1%)
    pallas_call x8, Pallas kernels, exchange(): pl.pallas_call(lambda *refs: exchange_kernel(kinds, n_group, scratch_coun...  204 us
    dot_general x45, matrix products, mm(): lax.dot_general(left, right, (dims, ((), ())), preferred_element_type=jnp...  81.6 us

commit v1 on v0

--- a/solution.py
+++ b/solution.py
@@ -463,8 +463,13 @@
     before_grad_b = grad_before.astype(bf16)
     second_part = mm(before_grad_b, w_expand, NT).astype(bf16)
 
-    (second_parts,) = exchange(
-        3, ("za2a", second_part.reshape(group_count, token_count, width))
+    expand_term = mm(all_second, before_grad_b, TN).astype(bf16)
+    reduce_term = mm(all_cotan, active, TN).astype(bf16)
+    second_parts, expand_total, reduce_total = exchange(
+        3,
+        ("za2a", second_part.reshape(group_count, token_count, width)),
+        ("dpscatter", expand_term[None]),
+        ("dpscatter", reduce_term[None]),
     )
     grad_second = jnp.sum(second_parts.astype(jnp.float32), axis=0)
     grad_middle = cotangent + norm_backward(
@@ -495,14 +500,10 @@
     key_grad_b = key_grad.astype(bf16)
     value_grad_b = value_grad.astype(bf16)
 
-    ffn_terms = jnp.stack(
-        [mm(all_second, before_grad_b, TN).astype(bf16), mm(all_cotan, active, TN).astype(bf16)]
-    )
-    left, right, ffn_total = exchange(
+    left, right = exchange(
         4,
         ("za2a", jnp.stack([hidden_first, hidden_first, hidden_first, attended])),
         ("za2a", jnp.stack([query_grad_b, key_grad_b, value_grad_b, middle_b])),
-        ("dpscatter", ffn_terms),
     )
     grad_first = (
         mm(query_grad_b, w_query, NT) + mm(key_grad_b, w_key, NT) + mm(value_grad_b, w_value, NT)
@@ -524,24 +525,25 @@
     bias_terms = jnp.where(owner_mask[:, None], jnp.sum(grad_before, axis=0)[None], 0.0)
     vector_terms = jnp.concatenate([small_terms, bias_terms.reshape(-1, width)], axis=0)
     attn_term = mm(left.reshape(-1, width), right.reshape(-1, width), TN).astype(bf16)
-    vector_all, attn_total = exchange(5, ("dpag", vector_terms), ("dpscatter", attn_term[None]))
+    vector_all, attn_total, out_parts = exchange(
+        5,
+        ("dpag", vector_terms),
+        ("dpscatter", attn_term[None]),
+        ("za2a", out_part.reshape(group_count, token_count, width)),
+    )
+    outputs = middle + jnp.sum(out_parts.astype(jnp.float32), axis=0) + vectors[7]
     total_tokens = float(token_count * dp_count * group_count)
     attn_grads = attn_total / total_tokens
-    ffn_grads = ffn_total / total_tokens
+    ffn_grads = jnp.concatenate([expand_total, reduce_total], axis=0) / total_tokens
     attn_next = momentum_rate * attn_momenta + attn_grads
     ffn_next = momentum_rate * ffn_momenta + ffn_grads
     own_next = jnp.concatenate([attn_next, ffn_next], axis=0)
     squares = jnp.sum(own_next * own_next, axis=(1, 2))
     squares = jnp.broadcast_to(jnp.pad(squares, (0, 5))[:, None], (8, 128))
 
-    next_full, square_all, vector_groups, out_parts = exchange(
-        6,
-        ("dprow", own_next.astype(bf16)),
-        ("dpag", squares),
-        ("zag", jnp.sum(vector_all, axis=0)),
-        ("za2a", out_part.reshape(group_count, token_count, width)),
-    )
-    outputs = middle + jnp.sum(out_parts.astype(jnp.float32), axis=0) + vectors[7]
+    next_full, square_all, vector_groups = exchange(
+        6, ("dprow", own_next.astype(bf16)), ("dpag", squares), ("zag", jnp.sum(vector_all, axis=0))
+    )
     square_plane = jnp.sum(square_all, axis=0)
     own_b = own_next.astype(bf16)
     gram_part = jnp.concatenate([mm(own_b[1], next_full[1], NT), mm(own_b[2], next_full[2], NT)])

time: 340 us -> 350 us (1.029)
  matrix products: 83.7 us -> 88.6 us
    dot_general x45, matrix products: 81.6 us -> 85.3 us  [mm(): lax.dot_general(left, right, (dims, ((), ())), preferred_element_type=jnp...]
where the time goes in v1:
time: 350 us; the launch traced here: 344 us
  Pallas kernels  206 us (59%)
  matrix products  88.6 us (25%)
  other arithmetic  32 us (9%)
  local copies, waits for them, and re-layouts  13.7 us (4%)
  between operations  3.85 us (1%)
    pallas_call x8, Pallas kernels, exchange(): pl.pallas_call(lambda *refs: exchange_kernel(kinds, n_group, scratch_coun...  206 us
    dot_general x45, matrix products, mm(): lax.dot_general(left, right, (dims, ((), ())), preferred_element_type=jnp...  85.3 us

profile of v1, /device:TPU:0, one launch (start us, length us, event | category | flops | bytes accessed | tf_op | source)
XLA Modules:
  0.0 344.2 jit_solution(6621614116092911151)
XLA Ops:
  0.7 1.7 slice_reduce_fusion
  4.7 2.4 fusion.186
  7.1 1.8 convert_element_type.284.refs_1_
  9.6 41.7 %exchange_0.1 = (bf16[4,768,768]{2,1,0:T(8,128)(2,1)}, bf16[2,768,768]{2,1,0:T(8,128)(2,1)}, bf16[4,128,768]{2,1,0:T(8,128)(2,1)}) custom-call(bf16[96,768]{1,0:T(8,128)(2,1)} %convert_bitcast_fusion.refs_0_, bf16[2,96,768]{2,1,0:T(8,128)(2,1)} %convert_element_type.284.refs_1_, bf16[128,768]{1,0:T(8,128)(2,1)} %get-tuple-element.72.refs_2_), custom_call_target="tpu_custom_call" | custom-call | tf_op jit(solution)/shard_map/exchange_0/pallas_call | solution.py:350
  51.3 1.7 fusion.46
  53.1 1.6 fusion.49
  55.8 1.6 fusion.55
  57.9 1.7 fusion.191
  60.7 19.4 %exchange_2.1 = bf16[4,128,768]{2,1,0:T(8,128)(2,1)} custom-call(bf16[128,768]{1,0:T(8,128)(2,1)} %add_convert_fusion.refs_0_), custom_call_target="tpu_custom_call" | custom-call | tf_op jit(solution)/shard_map/exchange_2/pallas_call | solution.py:350
  80.3 2.4 convolution_add_fusion
  82.7 1.9 fusion.5.refs_2_
  85.3 1.4 fusion.192
  86.7 1.9 fusion.4.refs_1_
  88.6 1.7 convolution_convert_fusion.3
  90.3 23.9 %exchange_3.1 = (bf16[4,128,768]{2,1,0:T(8,128)(2,1)}, f32[1,96,768]{2,1,0:T(8,128)}, f32[1,96,768]{2,1,0:T(8,128)}) custom-call(bf16[4,128,768]{2,1,0:T(8,128)(2,1)} %bitcast.203, bf16[1,768,768]{2,1,0:T(8,128)(2,1)} %fusion.4.refs_1_, bf16[1,768,768]{2,1,0:T(8,128)(2,1)} %fusion.5.refs_2_), custom_call_target="tpu_custom_call" | custom-call | tf_op jit(solution)/shard_map/exchange_3/pallas_call | solution.py:350
  114.2 2.0 multiply_add_fusion.14
  118.8 2.5 fusion.52
  122.4 1.7 fusion.187
  124.1 1.7 copy.61
  127.4 2.1 pad_maximum_fusion.2.refs_1_
  130.8 37.2 %exchange_4.1 = (bf16[4,128,768]{2,1,0:T(8,128)(2,1)}, bf16[4,128,768]{2,1,0:T(8,128)(2,1)}) custom-call(bf16[4,128,768]{2,1,0:T(8,128)(2,1)} %pad_maximum_fusion.1.refs_0_, bf16[4,128,768]{2,1,0:T(8,128)(2,1)} %pad_maximum_fusion.2.refs_1_), custom_call_target="tpu_custom_call" | custom-call | tf_op jit(solution)/shard_map/exchange_4/pallas_call | solution.py:350
  168.0 3.5 %fusion.6.refs_1_ = bf16[1,768,768]{2,1,0:T(8,128)(2,1)} fusion(bf16[4,128,768]{2,1,0:T(8,128)(2,1)} %get-tuple-element.31, bf16[4,128,768]{2,1,0:T(8,128)(2,1)} %get-tuple-element.32), kind=kOutput, calls=%fused_computation.36 | convolution fusion | flops 604569600 | bytes 2752512 | tf_op jit(solution)/shard_map/dot_general | solution.py:366
  171.5 1.8 fusion.33
  173.4 1.8 convolution_add_fusion.2
  175.2 1.9 multiply_reduce_fusion.2
  178.5 1.3 concatenate.13.refs_0_
  179.7 3.5 %convolution_convert_fusion.2 = bf16[512,768]{1,0:T(8,128)(2,1)} fusion(bf16[2,768,768]{2,1,0:T(8,128)(2,1)} %get-tuple-element.28, f32[512,768]{1,0:T(8,128)} %copy-done.14), kind=kOutput, calls=%fused_computation.37 | convolution fusion | flops 605159424 | bytes 3538944 | tf_op jit(solution)/shard_map/dot_general | solution.py:366
  183.2 24.4 %exchange_5.1 = (f32[8,12,768]{2,1,0:T(8,128)}, f32[1,96,768]{2,1,0:T(8,128)}, bf16[4,128,768]{2,1,0:T(8,128)(2,1)}) custom-call(f32[12,768]{1,0:T(8,128)} %concatenate.13.refs_0_, bf16[1,768,768]{2,1,0:T(8,128)(2,1)} %fusion.6.refs_1_, bf16[4,128,768]{2,1,0:T(8,128)(2,1)} %bitcast.202), custom_call_target="tpu_custom_call" | custom-call | tf_op jit(solution)/shard_map/exchange_5/pallas_call | solution.py:350
  207.7 1.8 multiply_add_fusion.17
  211.8 24.7 %exchange_6.1 = (bf16[3,768,768]{2,1,0:T(8,128)(2,1)}, f32[8,8,128]{2,1,0:T(8,128)}, f32[4,12,768]{2,1,0:T(8,128)}) custom-call(bf16[3,96,768]{2,1,0:T(8,128)(2,1)} %fusion.100.refs_0_, f32[8,128]{1,0:T(8,128)} %broadcast_in_dim.50.refs_1_, f32[12,768]{1,0:T(8,128)} %reduce_sum.284.refs_2_), custom_call_target="tpu_custom_call" | custom-call | tf_op jit(solution)/shard_map/exchange_6/pallas_call | solution.py:350
  236.5 1.9 fusion.68
  238.4 1.9 fusion.71
  241.6 13.0 %exchange_7.1 = (bf16[4,48,768]{2,1,0:T(8,128)(2,1)}, f32[4,8,128]{2,1,0:T(8,128)}) custom-call(bf16[4,48,768]{2,1,0:T(8,128)(2,1)} %bitcast.195, f32[8,128]{1,0:T(8,128)} %reduce_sum.286.refs_1_), custom_call_target="tpu_custom_call" | custom-call | tf_op jit(solution)/shard_map/exchange_7/pallas_call | solution.py:350
  258.9 21.6 %exchange_8.1 = bf16[2,768,768]{2,1,0:T(8,128)(2,1)} custom-call(bf16[48,768]{1,0:T(8,128)(2,1)} %multiply_convert_fusion.14.refs_0_), custom_call_target="tpu_custom_call" | custom-call | tf_op jit(solution)/shard_map/exchange_8/pallas_call | solution.py:350
  280.5 3.2 fusion
  286.3 1.4 copy-done.2
  288.9 1.5 convolution_add_fusion.9
  293.0 1.4 copy-done
  295.4 4.4 %fusion.61 = f32[1,96,768]{2,1,0:T(8,128)} fusion(f32[]{:T(128)} %bitcast.44, bf16[3,768,768]{2,1,0:T(8,128)(2,1)} %get-tuple-element.40, f32[768,768]{1,0:T(8,128)} %copy-done, f32[2,96,768]{2,1,0:T(8,128)S(1)} %get-tuple-element.65, f32[96,768]{1,0:T(8,128)} %convolution_add_fusion.8, f32[96,768]{1,0:T(8,128)} %copy-done.8), kind=kOutput, calls=%fused_computation.95 | convolution fusion | flops 229588992 | bytes 5014528 | tf_op jit(solution)/shard_map/dot_general | solution.py:366
  299.9 10.6 %fusion.2 = f32[768,768]{1,0:T(8,128)S(1)} fusion(bf16[2,768,768]{2,1,0:T(8,128)(2,1)S(1)} %copy-done.11), kind=kOutput, calls=%fused_computation.6 | convolution fusion | flops 908328960 | bytes 4718592 | tf_op jit(solution)/shard_map/dot_general | solution.py:366
  317.5 3.6 %fusion.59 = f32[1,96,768]{2,1,0:T(8,128)} fusion(f32[]{:T(128)} %bitcast.46, bf16[3,768,768]{2,1,0:T(8,128)(2,1)} %get-tuple-element.40, f32[768,768]{1,0:T(8,128)S(1)} %multiply_add_fusion, f32[2,96,768]{2,1,0:T(8,128)S(1)} %get-tuple-element.65, f32[96,768]{1,0:T(8,128)} %convolution_add_fusion.6, f32[96,768]{1,0:T(8,128)} %copy-done.9), kind=kOutput, calls=%fused_computation.93 | convolution fusion | flops 229588992 | bytes 5014528 | tf_op jit(solution)/shard_map/dot_general | solution.py:366
  321.1 2.1 fusion.102
  323.2 1.5 multiply_reduce_fusion.10
  324.8 1.5 multiply_subtract_fusion
  326.3 1.2 slice.109
  328.2 2.8 fusion.98
  339.1 2.8 fusion.67
  341.9 1.3 convert_reduce_fusion.2
  (176 shorter events, 43.6 us)
Async XLA Ops:
  0.6 50.7 %copy-start.1 = (f32[128,768]{1,0:T(8,128)S(1)}, f32[128,768]{1,0:T(8,128)}, u32[]{:S(2)}) copy-start(f32[128,768]{1,0:T(8,128)} %param.9) | copy-start | bytes 1179652
  0.7 8.3 %copy-start.16 = (f32[1,96,768]{2,1,0:T(8,128)S(1)}, f32[1,96,768]{2,1,0:T(8,128)}, u32[]{:S(2)}) copy-start(f32[1,96,768]{2,1,0:T(8,128)} %param.12) | copy-start | bytes 884740
  2.4 53.5 %copy-start.29 = (f32[768]{0:T(1024)}, f32[768]{0:T(1024)S(1)}, u32[]{:S(2)}) copy-start(f32[768]{0:T(1024)S(1)} %get-tuple-element.58) | copy-start | bytes 9220
  3.5 52.4 %copy-start.36 = (f32[128]{0:T(128)}, f32[128]{0:T(128)S(1)}, u32[]{:S(2)}) copy-start(f32[128]{0:T(128)S(1)} %broadcast_multiply_fusion.7) | copy-start | bytes 1540
  4.7 51.2 %copy-start.41 = (f32[128]{0:T(128)}, f32[128]{0:T(128)S(1)}, u32[]{:S(2)}) copy-start(f32[128]{0:T(128)S(1)} %add_rsqrt_fusion.1) | copy-start | bytes 1540
  51.3 3.7 %copy-start.45 = (s32[1,4]{1,0:T(1,128)S(1)}, s32[1,4]{1,0:T(1,128)}, u32[]{:S(2)}) copy-start(s32[1,4]{1,0:T(1,128)} %param.11) | copy-start | bytes 52
  57.7 22.4 %copy-start.12 = (bf16[128,768]{0,1:T(8,128)(2,1)}, bf16[128,768]{0,1:T(8,128)(2,1)S(1)}, u32[]{:S(2)}) copy-start(bf16[128,768]{0,1:T(8,128)(2,1)S(1)} %copy.50) | copy-start | bytes 589828
  57.9 22.2 %slice-start = ((f32[12,768]{1,0:T(8,128)}), f32[4,768]{1,0:T(4,128)S(1)}, s32[]{:S(2)}) async-start(f32[12,768]{1,0:T(8,128)} %param.16), calls=%async_computation | async-start | bytes 24576 | tf_op jit(solution)/shard_map/slice | solution.py:458
  59.7 20.5 %copy-start.34 = (f32[128]{0:T(128)}, f32[128]{0:T(128)S(1)}, u32[]{:S(2)}) copy-start(f32[128]{0:T(128)S(1)} %broadcast_multiply_fusion.6) | copy-start | bytes 1540
  59.9 20.3 %copy-start.38 = (f32[128]{0:T(128)}, f32[128]{0:T(128)S(1)}, u32[]{:S(2)}) copy-start(f32[128]{0:T(128)S(1)} %add_rsqrt_fusion) | copy-start | bytes 1540
  80.1 2.5 copy-start.17
  82.6 4.1 %copy-start.14 = (f32[512,768]{1,0:T(8,128)}, f32[512,768]{1,0:T(8,128)S(1)}, u32[]{:S(2)}) copy-start(f32[512,768]{1,0:T(8,128)S(1)} %convolution_add_fusion) | copy-start | bytes 4718596
  82.6 2.7 copy-start.44
  85.3 1.4 copy-start.20
  90.3 24.0 %copy-start.21 = (f32[2,96,768]{2,1,0:T(8,128)S(1)}, f32[2,96,768]{2,1,0:T(8,128)}, u32[]{:S(2)}) copy-start(f32[2,96,768]{2,1,0:T(8,128)} %param.15) | copy-start | bytes 1769476
  114.2 2.1 copy-start.19
  114.2 3.0 copy-start.35
  114.2 3.0 copy-start.39
  114.2 3.7 %copy-start.15 = (f32[128,768]{1,0:T(8,128)S(1)}, f32[128,768]{1,0:T(8,128)}, u32[]{:S(2)}) copy-start(f32[128,768]{1,0:T(8,128)} %param.10) | copy-start | bytes 1179652
  116.3 201.2 %copy-start.4 = (f32[2,96,768]{2,1,0:T(8,128)}, f32[2,96,768]{2,1,0:T(8,128)S(1)}, u32[]{:S(2)}) copy-start(f32[2,96,768]{2,1,0:T(8,128)S(1)} %get-tuple-element.65) | copy-start | bytes 1769476
  118.8 7.0 %copy-start.13 = (bf16[128,768]{0,1:T(8,128)(2,1)S(1)}, bf16[128,768]{0,1:T(8,128)(2,1)}, u32[]{:S(2)}) copy-start(bf16[128,768]{0,1:T(8,128)(2,1)} %copy-done.12) | copy-start | bytes 589828
  126.4 3.3 copy-start.30
  126.4 3.3 copy-start.37
  126.4 3.3 copy-start.42
  171.5 3.7 %copy-start.18 = (bf16[128,12,64]{0,2,1:T(8,128)(2,1)S(1)}, bf16[128,12,64]{0,2,1:T(8,128)(2,1)}, u32[]{:S(2)}) copy-start(bf16[128,12,64]{0,2,1:T(8,128)(2,1)} %get-tuple-element.74) | copy-start | bytes 589828
  171.5 3.7 %copy-start.43 = (f32[128]{0:T(128)S(1)}, f32[128]{0:T(128)}, u32[]{:S(2)}) copy-start(f32[128]{0:T(128)} %copy-done.41) | copy-start | bytes 1540
  175.2 3.0 copy-start.26
  175.2 3.1 copy-start.33
  175.2 3.1 copy-start.32
  175.2 3.2 copy-start.40
  175.2 3.2 copy-start.31
  179.7 27.9 %copy-start.23 = (f32[1,96,768]{2,1,0:T(8,128)S(1)}, f32[1,96,768]{2,1,0:T(8,128)}, u32[]{:S(2)}) copy-start(f32[1,96,768]{2,1,0:T(8,128)} %param.13) | copy-start | bytes 884740
  207.7 3.5 %copy-start.22 = (f32[8,12,768]{2,1,0:T(8,128)S(1)}, f32[8,12,768]{2,1,0:T(8,128)}, u32[]{:S(2)}) copy-start(f32[8,12,768]{2,1,0:T(8,128)} %get-tuple-element.37) | copy-start | bytes 884740
  209.5 0.9 copy-start.5
  236.5 4.5 %copy-start.27 = (f32[8,8,128]{2,1,0:T(8,128)S(1)}, f32[8,8,128]{2,1,0:T(8,128)}, u32[]{:S(2)}) copy-start(f32[8,8,128]{2,1,0:T(8,128)} %get-tuple-element.39) | copy-start | bytes 98308
  280.5 3.3 copy-start.10
  283.8 1.5 copy-start.7
  286.3 1.4 copy-start.2
  288.9 1.8 copy-start.3
  290.7 2.2 copy-start.8
  293.0 1.4 copy-start
  295.4 4.4 %copy-start.11 = (bf16[2,768,768]{2,1,0:T(8,128)(2,1)S(1)}, bf16[2,768,768]{2,1,0:T(8,128)(2,1)}, u32[]{:S(2)}) copy-start(bf16[2,768,768]{2,1,0:T(8,128)(2,1)} %exchange_8.1) | copy-start | bytes 7077892
  314.2 2.2 copy-start.9
  317.5 5.7 %copy-start.24 = (f32[4,12,768]{2,1,0:T(8,128)S(1)}, f32[4,12,768]{2,1,0:T(8,128)}, u32[]{:S(2)}) copy-start(f32[4,12,768]{2,1,0:T(8,128)} %get-tuple-element.38) | copy-start | bytes 442372
  324.8 6.2 %copy-start.25 = (f32[12,768]{1,0:T(8,128)}, f32[12,768]{1,0:T(8,128)S(1)}, u32[]{:S(2)}) copy-start(f32[12,768]{1,0:T(8,128)S(1)} %get-tuple-element.61) | copy-start | bytes 110596
  338.0 1.1 copy-start.6
  339.1 4.1 %copy-start.28 = (f32[768]{0:T(1024)S(1)}, f32[768]{0:T(1024)}, u32[]{:S(2)}) copy-start(f32[768]{0:T(1024)} %get-tuple-element.52) | copy-start | bytes 9220
